TPU v7x, 32 devices: a whole 2x2x4 slice. The times are simulated.
32 devices in a mesh: mem: 4 (over x, core), grid: 8 (over z, y).
Axes of the slice: x: 2, y: 2, z: 4, core: 2. Of those that a mesh axis runs over, the one named last changes fastest.
Arguments:
- obs_ensemble: bfloat16 [256, 32, 256], P('mem', 'grid'), may hold values from -6 to 6
- obs_values: bfloat16 [32, 256], P('grid'), may hold values from -6 to 6
- inverse_error: bfloat16 [32, 256], P('grid'), may hold values from 0.5 to 8
- obs_counts: int32 [32], P('grid'), may hold values from 1 to 256, as said below
- loc_offsets: int32 [32, 4], P('grid'), may hold values from -2 to 2, as said below
- background: bfloat16 [256, 256, 320], P('mem', 'grid'), may hold values from -6 to 6
Outputs:
- analysis: bfloat16 [256, 256, 320], P('mem', 'grid')
Inputs may be any that keep to these rules, and one draw needn't show every extreme that they name: `obs_counts`: counts up to about five times their mean; some block in every draw is full. `loc_offsets`: entry 0 of every list is 0 (the block's own observations); the other entries of a list are distinct nonzero offsets.
All inputs are finite; a program needn't handle non-finite values.
Results may differ from a plain program's by a relative error of at most 0.0063.
Values may be sent and summed in bfloat16 or wider, within the bound.
A program may use at most 128 MiB of HBM per device.

v0:
```python
import jax
import jax.numpy as jnp
from jax import lax
from jax.sharding import PartitionSpec as P

MEMBERS = 256
BLOCK_COLS = 8
REACH = 2
LOC_LEN = 4
NS_STEPS = 6


def padded(x, sides, width):
    for axis, dim in sides:
        count, length = (lax.axis_size(axis), x.shape[dim])
        up = [(i, (i + 1) % count) for i in range(count)]
        down = [(j, i) for i, j in up]
        last = lax.slice_in_dim(x, length - width, length, axis=dim)
        initial = lax.slice_in_dim(x, 0, width, axis=dim)
        before = lax.ppermute(last, axis, up)
        after = lax.ppermute(initial, axis, down)
        x = jnp.concatenate([before, x, after], axis=dim)
    return x


def taper_of(offsets):
    return 1.0 / (1.0 + jnp.abs(offsets).astype(jnp.float32))


def block_weights(members, obs_row, weight_row):
    members_wide = members.astype(jnp.float32)
    obs_mean = jnp.mean(members_wide, axis=0)
    scaled = ((members_wide - obs_mean) * weight_row).astype(jnp.bfloat16)
    innovation = (obs_row - obs_mean) * weight_row
    gram = jnp.dot(scaled, scaled.T, preferred_element_type=jnp.float32)
    rhs = jnp.dot(scaled.astype(jnp.float32), innovation, precision=lax.Precision.HIGHEST)
    identity = jnp.eye(MEMBERS, dtype=jnp.float32)
    system = identity + gram / (MEMBERS - 1)
    scale = jnp.sqrt(jnp.sum(system * system))
    upper = system / scale
    lower = identity
    for step in range(NS_STEPS):
        middle = 0.5 * (3.0 * identity - jnp.dot(lower, upper, precision=lax.Precision.HIGHEST))
        upper = jnp.dot(upper, middle, precision=lax.Precision.HIGHEST)
        lower = jnp.dot(middle, lower, precision=lax.Precision.HIGHEST)
    root_inv = lower / jnp.sqrt(scale)
    inner = jnp.dot(root_inv, rhs, precision=lax.Precision.HIGHEST)
    shift = jnp.dot(root_inv, inner, precision=lax.Precision.HIGHEST) / (MEMBERS - 1)
    return (root_inv + shift[:, None]).astype(jnp.bfloat16)


def apply_weights(weights, state):
    state_wide = state.astype(jnp.float32)
    state_mean = jnp.mean(state_wide, axis=0)
    perturbation = (state_wide - state_mean).astype(jnp.bfloat16)
    product = jnp.einsum("bkj,kbv->jbv", weights, perturbation, preferred_element_type=jnp.float32)
    return (state_mean + product).astype(jnp.bfloat16)


def on_device(obs_ensemble, obs_values, inverse_error, obs_counts, loc_offsets, background):
    local_members, dev_blocks, slots = obs_ensemble.shape
    mem_count = lax.axis_size("mem")
    per_device = dev_blocks // mem_count
    list_width = LOC_LEN * slots
    slot_ids = jnp.arange(slots, dtype=jnp.int32)
    valid = (slot_ids[None, :] < obs_counts[:, None]).astype(jnp.float32)
    masked = (inverse_error.astype(jnp.float32) * valid).astype(jnp.bfloat16)
    stacked = jnp.concatenate([obs_ensemble, obs_values[None], masked[None]], axis=0)
    extended = padded(stacked, (("grid", 1),), REACH)
    chosen = (jnp.arange(dev_blocks, dtype=jnp.int32)[:, None] + REACH + loc_offsets).reshape(-1)
    picked = jnp.take(extended, chosen, axis=1).reshape(local_members + 2, dev_blocks, list_width)
    member_part = picked[:local_members].reshape(local_members, mem_count, per_device, list_width)
    mem_rank = lax.axis_index("mem")
    first_block = mem_rank * per_device
    table_part = lax.dynamic_slice_in_dim(picked[local_members:], first_block, per_device, 1)
    own_taper = lax.dynamic_slice_in_dim(taper_of(loc_offsets), first_block, per_device, 0)
    taper_rows = jnp.repeat(own_taper, slots, axis=1)
    received = lax.all_to_all(member_part, "mem", split_axis=1, concat_axis=0, tiled=True)
    received = received.reshape(MEMBERS, per_device, list_width)
    weight_rows = table_part[1].astype(jnp.float32) * taper_rows
    weights = jax.vmap(block_weights, in_axes=(1, 0, 0))(
        received, table_part[0].astype(jnp.float32), weight_rows
    )
    dev_cols = background.shape[1]
    variables = background.shape[2]
    pieces = background.reshape(local_members, mem_count, per_device * BLOCK_COLS, variables)
    moved = lax.all_to_all(pieces, "mem", split_axis=1, concat_axis=0, tiled=True)
    moved = moved.reshape(MEMBERS, per_device, BLOCK_COLS * variables)
    updated = apply_weights(weights, moved)
    updated = updated.reshape(MEMBERS, 1, per_device * BLOCK_COLS, variables)
    returned = lax.all_to_all(updated, "mem", split_axis=0, concat_axis=1, tiled=True)
    return returned.reshape(local_members, dev_cols, variables)


def solution(mesh):
    placed = (
        P("mem", "grid", None),
        P("grid", None),
        P("grid", None),
        P("grid"),
        P("grid", None),
        P("mem", "grid", None),
    )
    return jax.shard_map(
        on_device, mesh=mesh, in_specs=placed, out_specs=P("mem", "grid", None), check_vma=False
    )
```

profile of v0, /device:TPU:0, one launch (start us, length us, event | category | flops | bytes accessed | tf_op | source)
XLA Modules:
  0.0 82.5 jit_solution(6703048874097502343)
XLA Ops:
  0.0 0.8 fusion.21
  0.8 0.7 copy.22
  1.4 0.9 %copy.21 = bf16[64,4,256]{2,0,1:T(8,128)(2,1)S(1)} copy(bf16[64,4,256]{2,1,0:T(4,128)(2,1)} %param.6) | data formatting | bytes 262144 | tf_op args[0]
  2.4 3.0 %collective-permute-start = (bf16[66,2,256]{2,0,1:T(8,128)(2,1)S(1)}, bf16[66,2,256]{2,0,1:T(8,128)(2,1)S(1)}, u32[]{:S(2)}, u32[]{:S(2)}) collective-permute-start(bf16[66,2,256]{2,0,1:T(8,128)(2,1)S(1)} %get-tuple-element.5), channel_id=1, source_target_pairs={{0,1},{1,2},{2,3},{3,4},{4,5},{5,6},{6,7},{7,0},{8,9},{9,10},{10,1... | collective-permute-start | bytes 202760 | tf_op jit(solution)/shard_map/ppermute | solution.py:20
  5.5 3.1 %collective-permute-start.1 = (bf16[66,2,256]{2,0,1:T(8,128)(2,1)S(1)}, bf16[66,2,256]{2,0,1:T(8,128)(2,1)S(1)}, u32[]{:S(2)}, u32[]{:S(2)}) collective-permute-start(bf16[66,2,256]{2,0,1:T(8,128)(2,1)S(1)} %get-tuple-element.6), channel_id=1, source_target_pairs={{1,0},{2,1},{3,2},{4,3},{5,4},{6,5},{7,6},{0,7},{9,8},{10,9},{11,1... | collective-permute-start | bytes 202760 | tf_op jit(solution)/shard_map/ppermute | solution.py:21
  8.6 0.8 broadcast_add_fusion
  9.5 1.3 %collective-permute-done = bf16[66,2,256]{2,0,1:T(8,128)(2,1)S(1)} collective-permute-done((bf16[66,2,256]{2,0,1:T(8,128)(2,1)S(1)}, bf16[66,2,256]{2,0,1:T(8,128)(2,1)S(1)}, u32[]{:S(2)}, u32[]{:S(2)}) %collective-permute-start) | collective-permute-done | bytes 67616 | tf_op jit(solution)/shard_map/ppermute | solution.py:20
  10.9 0.5 collective-permute-done.1
  11.4 0.6 gather_fusion
  12.7 0.9 %copy.25 = bf16[64,4,1,1024]{3,0,2,1:T(8,128)(2,1)} copy(bf16[64,4,1,1024]{3,1,0,2:T(4,128)(2,1)S(1)} %reshape.380) | data formatting | bytes 1048576 | tf_op jit(solution)/shard_map/reshape | solution.py:72
  13.7 3.5 %all-to-all-start.1 = ((bf16[64,4,1,1024]{3,0,2,1:T(8,128)(2,1)}), bf16[64,4,1,1024]{3,0,2,1:T(8,128)(2,1)S(1)}, u32[]{:S(2)}, u32[]{:S(2)}) async-start(bf16[64,4,1,1024]{3,0,2,1:T(8,128)(2,1)} %copy.25), calls=%async_computation.1 | async-start | bytes 1048576 | tf_op jit(solution)/shard_map/all_to_all | solution.py:78
  17.3 2.7 %copy.20 = bf16[64,4,8,320]{3,2,0,1:T(8,128)(2,1)} copy(bf16[64,4,8,320]{3,2,1,0:T(8,128)(2,1)} %bitcast.102) | data formatting | bytes 2621440 | tf_op jit(solution)/shard_map/reshape | solution.py:86
  20.1 5.9 %all-to-all-done.1 = bf16[64,4,1,1024]{3,0,2,1:T(8,128)(2,1)S(1)} async-done(((bf16[64,4,1,1024]{3,0,2,1:T(8,128)(2,1)}), bf16[64,4,1,1024]{3,0,2,1:T(8,128)(2,1)S(1)}, u32[]{:S(2)}, u32[]{:S(2)}) %all-to-all-start.1) | async-done | bytes 524320 | tf_op jit(solution)/shard_map/all_to_all | solution.py:78
  25.9 3.6 %all-to-all-start = ((bf16[64,4,8,320]{3,2,0,1:T(8,128)(2,1)}), bf16[64,4,8,320]{3,2,0,1:T(8,128)(2,1)S(1)}, u32[]{:S(2)}, u32[]{:S(2)}) async-start(bf16[64,4,8,320]{3,2,0,1:T(8,128)(2,1)} %copy.20), calls=%async_computation | async-start | bytes 3145728 | tf_op jit(solution)/shard_map/all_to_all | solution.py:87
  29.7 0.9 %multiply_reduce_fusion = (f32[]{:T(128)}, f32[256,256]{1,0:T(8,128)S(1)}) fusion(bf16[256,1024]{1,0:T(8,128)(2,1)S(1)} %bitcast.100), kind=kOutput, calls=%fused_computation.34 | convolution fusion | flops 134610944 | bytes 786436 | tf_op jit(solution)/shard_map/vmap()/dot_general | solution.py:35
  31.6 0.4 fusion.15
  37.3 0.5 convolution_bitcast_fusion.2
  38.9 10.6 %all-to-all-done = bf16[64,4,8,320]{3,2,0,1:T(8,128)(2,1)S(1)} async-done(((bf16[64,4,8,320]{3,2,0,1:T(8,128)(2,1)}), bf16[64,4,8,320]{3,2,0,1:T(8,128)(2,1)S(1)}, u32[]{:S(2)}, u32[]{:S(2)}) %all-to-all-start) | async-done | bytes 1310752 | tf_op jit(solution)/shard_map/all_to_all | solution.py:87
  49.9 1.9 %convert_bitcast_fusion = f32[4,64,1,8,320]{4,3,1,0,2:T(8,128)} fusion(bf16[64,4,8,320]{3,2,0,1:T(8,128)(2,1)S(1)} %all-to-all-done), kind=kLoop, calls=%fused_computation.3 | loop fusion | flops 655360 | bytes 3932160 | tf_op jit(solution)/shard_map/convert_element_type | solution.py:53
  51.8 2.9 %reshape.383 = f32[256,2560]{1,0:T(8,128)S(1)} reshape(f32[4,64,1,8,320]{4,3,1,0,2:T(8,128)} %convert_bitcast_fusion) | data formatting | bytes 5242880 | tf_op jit(solution)/shard_map/convert_element_type | solution.py:53
  54.7 1.9 %fusion.1 = bf16[1,2560,256]{2,1,0:T(8,128)(2,1)} fusion(f32[256,2560]{1,0:T(8,128)S(1)} %reshape.383, f32[2560]{0:T(1024)S(1)} %div.51, f32[256,256]{1,0:T(8,128)S(1)} %convolution_divide_fusion, f32[256]{0:T(256)S(1)} %broadcast_multiply_fusion.2), kind=kOutput, calls=%fused_computation.5 | convolution fusion | flops 338296832 | bytes 4205568 | tf_op jit(solution)/shard_map/bkj,kbv->jbv/dot_general | solution.py:56
  56.6 2.1 %copy.28 = bf16[256,1,8,320]{3,2,1,0:T(8,128)(2,1)S(1)} copy(bf16[256,1,8,320]{0,3,2,1:T(8,128)(2,1)} %bitcast.99) | data formatting | bytes 2621440 | tf_op jit(solution)/shard_map/reshape | solution.py:90
  58.7 22.5 %all_to_all.33 = bf16[256,1,8,320]{3,2,1,0:T(8,128)(2,1)S(1)} all-to-all(bf16[256,1,8,320]{3,2,1,0:T(8,128)(2,1)S(1)} %copy.28), channel_id=1, replica_groups=mesh['mem'=4,'grid'=8] {'mem'}, dimensions={0} | all-to-all | bytes 2621440 | tf_op jit(solution)/shard_map/all_to_all | solution.py:91
  81.2 1.3 %copy.31 = bf16[64,4,1,8,320]{4,3,1,0,2:T(8,128)(2,1)} copy(bf16[64,4,1,8,320]{4,3,0,1,2:T(8,128)(2,1)S(1)} %bitcast.98) | data formatting | bytes 2621440 | tf_op jit(solution)/shard_map/all_to_all | solution.py:91
  (49 shorter events, 8.2 us)
Async XLA Ops:
  2.4 8.5 %collective-permute-start = (bf16[66,2,256]{2,0,1:T(8,128)(2,1)S(1)}, bf16[66,2,256]{2,0,1:T(8,128)(2,1)S(1)}, u32[]{:S(2)}, u32[]{:S(2)}) collective-permute-start(bf16[66,2,256]{2,0,1:T(8,128)(2,1)S(1)} %get-tuple-element.5), channel_id=1, source_target_pairs={{0,1},{1,2},{2,3},{3,4},{4,5},{5,6},{6,7},{7,0},{8,9},{9,10},{10,1... | collective-permute-start | bytes 202760 | tf_op jit(solution)/shard_map/ppermute | solution.py:20
  5.5 5.9 %collective-permute-start.1 = (bf16[66,2,256]{2,0,1:T(8,128)(2,1)S(1)}, bf16[66,2,256]{2,0,1:T(8,128)(2,1)S(1)}, u32[]{:S(2)}, u32[]{:S(2)}) collective-permute-start(bf16[66,2,256]{2,0,1:T(8,128)(2,1)S(1)} %get-tuple-element.6), channel_id=1, source_target_pairs={{1,0},{2,1},{3,2},{4,3},{5,4},{6,5},{7,6},{0,7},{9,8},{10,9},{11,1... | collective-permute-start | bytes 202760 | tf_op jit(solution)/shard_map/ppermute | solution.py:21
  12.5 4.6 %copy-start = (s32[4,4]{1,0:T(4,128)S(1)}, s32[4,4]{1,0:T(4,128)}, u32[]{:S(2)}) copy-start(s32[4,4]{1,0:T(4,128)} %param.10) | copy-start | bytes 196
  13.7 12.3 %all-to-all-start.1 = ((bf16[64,4,1,1024]{3,0,2,1:T(8,128)(2,1)}), bf16[64,4,1,1024]{3,0,2,1:T(8,128)(2,1)S(1)}, u32[]{:S(2)}, u32[]{:S(2)}) async-start(bf16[64,4,1,1024]{3,0,2,1:T(8,128)(2,1)} %copy.25), calls=%async_computation.1 | async-start | bytes 1048576 | tf_op jit(solution)/shard_map/all_to_all | solution.py:78
  25.9 23.6 %all-to-all-start = ((bf16[64,4,8,320]{3,2,0,1:T(8,128)(2,1)}), bf16[64,4,8,320]{3,2,0,1:T(8,128)(2,1)S(1)}, u32[]{:S(2)}, u32[]{:S(2)}) async-start(bf16[64,4,8,320]{3,2,0,1:T(8,128)(2,1)} %copy.20), calls=%async_computation | async-start | bytes 3145728 | tf_op jit(solution)/shard_map/all_to_all | solution.py:87
where the time goes:
time: 83 us; the launch traced here: 82.5 us
  blocking collectives  22.5 us (27%)
  waiting for transfers between devices  18.4 us (22%)
  starting transfers between devices  13.2 us (16%)
  local copies, waits for them, and re-layouts  13.1 us (16%)
  matrix products  10.2 us (12%)
  other arithmetic  4.13 us (5%)
  between operations  1 us (1%)
    all_to_all x1, blocking collectives, on_device(): lax.all_to_all(updated, 'mem', split_axis=0, concat_axis=1, tiled=True)  22.5 us
    all_to_all x1, waiting for transfers between devices, on_device(): lax.all_to_all(pieces, 'mem', split_axis=1, concat_axis=0, tiled=True)  10.6 us
    all_to_all x1, waiting for transfers between devices, on_device(): lax.all_to_all(member_part, 'mem', split_axis=1, concat_axis=0, tiled=True)  5.87 us
    all_to_all x1, starting transfers between devices, on_device(): lax.all_to_all(pieces, 'mem', split_axis=1, concat_axis=0, tiled=True)  3.56 us
    all_to_all x1, starting transfers between devices, on_device(): lax.all_to_all(member_part, 'mem', split_axis=1, concat_axis=0, tiled=True)  3.47 us
    ppermute x1, starting transfers between devices, padded(): after = lax.ppermute(initial, axis, down)  3.1 us
    ppermute x1, starting transfers between devices, padded(): before = lax.ppermute(last, axis, up)  3.05 us
    convert_element_type x1, local copies, waits for them, and re-layouts, apply_weights(): state_wide = state.astype(jnp.float32)  2.9 us
  transfers between devices with their start and end apart: 4, of which 4 were waited for; matrix products, arithmetic and copies ran while one was open for 15% of the time, Pallas kernels for 0%

commit v1 on v0

--- a/solution.py
+++ b/solution.py
@@ -75,7 +75,12 @@
     table_part = lax.dynamic_slice_in_dim(picked[local_members:], first_block, per_device, 1)
     own_taper = lax.dynamic_slice_in_dim(taper_of(loc_offsets), first_block, per_device, 0)
     taper_rows = jnp.repeat(own_taper, slots, axis=1)
-    received = lax.all_to_all(member_part, "mem", split_axis=1, concat_axis=0, tiled=True)
+    received = jnp.concatenate(
+        lax.all_to_all(
+            jnp.stack(jnp.split(member_part, lax.axis_size("mem"), axis=1)), "mem", 0, 0
+        ),
+        axis=0,
+    )
     received = received.reshape(MEMBERS, per_device, list_width)
     weight_rows = table_part[1].astype(jnp.float32) * taper_rows
     weights = jax.vmap(block_weights, in_axes=(1, 0, 0))(

time: 83 us -> 83.8 us (level)
  other arithmetic: 4.13 us -> 4.98 us
    reshape x2 -> x1, local copies, waits for them, and re-layouts: 1.14 us -> 0.2 us  [on_device(): picked[:local_members]]
    another operation x0 -> x1, other arithmetic: none -> 0.86 us  [on_device(): jnp.stack(jnp.split(member_part, lax.axis_size('mem'), axis=1))]
where the time goes in v1:
time: 83.8 us; the launch traced here: 83.3 us
  blocking collectives  22.5 us (27%)
  waiting for transfers between devices  18.1 us (22%)
  starting transfers between devices  13.4 us (16%)
  local copies, waits for them, and re-layouts  13.1 us (16%)
  matrix products  10.2 us (12%)
  other arithmetic  4.98 us (6%)
  between operations  1.07 us (1%)
    all_to_all x1, blocking collectives, on_device(): lax.all_to_all(updated, 'mem', split_axis=0, concat_axis=1, tiled=True)  22.5 us
    all_to_all x1, waiting for transfers between devices, on_device(): lax.all_to_all(pieces, 'mem', split_axis=1, concat_axis=0, tiled=True)  10.4 us
    all_to_all x1, waiting for transfers between devices, on_device(): lax.all_to_all(jnp.stack(jnp.split(member_part, lax.axis_size('mem'), axi...  5.87 us
    all_to_all x1, starting transfers between devices, on_device(): lax.all_to_all(pieces, 'mem', split_axis=1, concat_axis=0, tiled=True)  3.74 us
    all_to_all x1, starting transfers between devices, on_device(): lax.all_to_all(jnp.stack(jnp.split(member_part, lax.axis_size('mem'), axi...  3.47 us
    ppermute x1, starting transfers between devices, padded(): after = lax.ppermute(initial, axis, down)  3.1 us
    ppermute x1, starting transfers between devices, padded(): before = lax.ppermute(last, axis, up)  3.05 us
    convert_element_type x1, local copies, waits for them, and re-layouts, apply_weights(): state_wide = state.astype(jnp.float32)  2.9 us
  transfers between devices with their start and end apart: 4, of which 4 were waited for; matrix products, arithmetic and copies ran while one was open for 15% of the time, Pallas kernels for 0%

profile of v1, /device:TPU:0, one launch (start us, length us, event | category | flops | bytes accessed | tf_op | source)
XLA Modules:
  0.0 83.3 jit_solution(4463727226949565383)
XLA Ops:
  0.0 0.8 fusion.20
  0.8 0.7 copy.51
  1.4 0.9 %copy.50 = bf16[64,4,256]{2,0,1:T(8,128)(2,1)S(1)} copy(bf16[64,4,256]{2,1,0:T(4,128)(2,1)} %param.6) | data formatting | bytes 262144 | tf_op args[0]
  2.4 3.0 %collective-permute-start = (bf16[66,2,256]{2,0,1:T(8,128)(2,1)S(1)}, bf16[66,2,256]{2,0,1:T(8,128)(2,1)S(1)}, u32[]{:S(2)}, u32[]{:S(2)}) collective-permute-start(bf16[66,2,256]{2,0,1:T(8,128)(2,1)S(1)} %get-tuple-element.9), channel_id=1, source_target_pairs={{0,1},{1,2},{2,3},{3,4},{4,5},{5,6},{6,7},{7,0},{8,9},{9,10},{10,1... | collective-permute-start | bytes 202760 | tf_op jit(solution)/shard_map/ppermute | solution.py:20
  5.5 3.1 %collective-permute-start.1 = (bf16[66,2,256]{2,0,1:T(8,128)(2,1)S(1)}, bf16[66,2,256]{2,0,1:T(8,128)(2,1)S(1)}, u32[]{:S(2)}, u32[]{:S(2)}) collective-permute-start(bf16[66,2,256]{2,0,1:T(8,128)(2,1)S(1)} %get-tuple-element.10), channel_id=1, source_target_pairs={{1,0},{2,1},{3,2},{4,3},{5,4},{6,5},{7,6},{0,7},{9,8},{10,9},{11,1... | collective-permute-start | bytes 202760 | tf_op jit(solution)/shard_map/ppermute | solution.py:21
  8.6 0.8 broadcast_add_fusion
  9.5 1.3 %collective-permute-done = bf16[66,2,256]{2,0,1:T(8,128)(2,1)S(1)} collective-permute-done((bf16[66,2,256]{2,0,1:T(8,128)(2,1)S(1)}, bf16[66,2,256]{2,0,1:T(8,128)(2,1)S(1)}, u32[]{:S(2)}, u32[]{:S(2)}) %collective-permute-start) | collective-permute-done | bytes 67616 | tf_op jit(solution)/shard_map/ppermute | solution.py:20
  10.9 0.5 collective-permute-done.1
  11.4 0.6 gather_fusion
  12.7 0.8 fusion.24
  13.7 0.9 %pad_maximum_fusion = bf16[4,64,1,1,1024]{4,1,3,2,0:T(8,128)(2,1)} fusion(bf16[1,64,1,1,1024]{4,1,3,2,0:T(8,128)(2,1)S(1)} %get-tuple-element.13, bf16[1,64,1,1,1024]{4,1,3,2,0:T(8,128)(2,1)S(1)} %get-tuple-element.14, bf16[1,64,1,1,1024]{4,1,3,2,0:T(8,128)(2,1)S(1)} %get-tuple-element.15, bf16[1,64,1,1,1024]{4,1,3,2,0:T(8,128)(2,1)S(1)} %get-tuple-element.16), kind=kLoop, calls=%fused_computation.31 | loop fusion | flops 786432 | bytes 1048576 | tf_op jit(solution)/shard_map/stack | solution.py:80
  14.5 3.5 %all-to-all-start.1 = ((bf16[4,64,1,1,1024]{4,1,3,2,0:T(8,128)(2,1)}), bf16[4,64,1,1,1024]{4,1,3,2,0:T(8,128)(2,1)S(1)}, u32[]{:S(2)}, u32[]{:S(2)}) async-start(bf16[4,64,1,1,1024]{4,1,3,2,0:T(8,128)(2,1)} %pad_maximum_fusion), calls=%async_computation.1 | async-start | bytes 1048576 | tf_op jit(solution)/shard_map/all_to_all | solution.py:79
  18.1 2.7 %copy.49 = bf16[64,4,8,320]{3,2,0,1:T(8,128)(2,1)} copy(bf16[64,4,8,320]{3,2,1,0:T(8,128)(2,1)} %bitcast.97) | data formatting | bytes 2621440 | tf_op jit(solution)/shard_map/reshape | solution.py:91
  20.9 5.9 %all-to-all-done.1 = bf16[4,64,1,1,1024]{4,1,3,2,0:T(8,128)(2,1)S(1)} async-done(((bf16[4,64,1,1,1024]{4,1,3,2,0:T(8,128)(2,1)}), bf16[4,64,1,1,1024]{4,1,3,2,0:T(8,128)(2,1)S(1)}, u32[]{:S(2)}, u32[]{:S(2)}) %all-to-all-start.1) | async-done | bytes 524320 | tf_op jit(solution)/shard_map/all_to_all | solution.py:79
  26.8 3.7 %all-to-all-start = ((bf16[64,4,8,320]{3,2,0,1:T(8,128)(2,1)}), bf16[64,4,8,320]{3,2,0,1:T(8,128)(2,1)S(1)}, u32[]{:S(2)}, u32[]{:S(2)}) async-start(bf16[64,4,8,320]{3,2,0,1:T(8,128)(2,1)} %copy.49), calls=%async_computation | async-start | bytes 3145728 | tf_op jit(solution)/shard_map/all_to_all | solution.py:92
  30.8 1.0 %multiply_reduce_fusion = (f32[]{:T(128)}, f32[256,256]{1,0:T(8,128)S(1)}) fusion(bf16[256,1024]{1,0:T(8,128)(2,1)S(1)} %bitcast.95), kind=kOutput, calls=%fused_computation.34 | convolution fusion | flops 134610944 | bytes 786436 | tf_op jit(solution)/shard_map/vmap()/dot_general | solution.py:35
  38.4 0.5 convolution_bitcast_fusion.2
  40.0 10.4 %all-to-all-done = bf16[64,4,8,320]{3,2,0,1:T(8,128)(2,1)S(1)} async-done(((bf16[64,4,8,320]{3,2,0,1:T(8,128)(2,1)}), bf16[64,4,8,320]{3,2,0,1:T(8,128)(2,1)S(1)}, u32[]{:S(2)}, u32[]{:S(2)}) %all-to-all-start) | async-done | bytes 1310752 | tf_op jit(solution)/shard_map/all_to_all | solution.py:92
  50.8 1.9 %convert_bitcast_fusion = f32[4,64,1,8,320]{4,3,1,0,2:T(8,128)} fusion(bf16[64,4,8,320]{3,2,0,1:T(8,128)(2,1)S(1)} %all-to-all-done), kind=kLoop, calls=%fused_computation.3 | loop fusion | flops 655360 | bytes 3932160 | tf_op jit(solution)/shard_map/convert_element_type | solution.py:53
  52.6 2.9 %reshape.380 = f32[256,2560]{1,0:T(8,128)S(1)} reshape(f32[4,64,1,8,320]{4,3,1,0,2:T(8,128)} %convert_bitcast_fusion) | data formatting | bytes 5242880 | tf_op jit(solution)/shard_map/convert_element_type | solution.py:53
  55.5 1.9 %fusion.1 = bf16[1,2560,256]{2,1,0:T(8,128)(2,1)} fusion(f32[256,2560]{1,0:T(8,128)S(1)} %reshape.380, f32[2560]{0:T(1024)S(1)} %div.51, f32[256,256]{1,0:T(8,128)S(1)} %convolution_divide_fusion, f32[256]{0:T(256)S(1)} %broadcast_multiply_fusion.2), kind=kOutput, calls=%fused_computation.5 | convolution fusion | flops 338296832 | bytes 4205568 | tf_op jit(solution)/shard_map/bkj,kbv->jbv/dot_general | solution.py:56
  57.4 2.1 %copy.55 = bf16[256,1,8,320]{3,2,1,0:T(8,128)(2,1)S(1)} copy(bf16[256,1,8,320]{0,3,2,1:T(8,128)(2,1)} %bitcast.94) | data formatting | bytes 2621440 | tf_op jit(solution)/shard_map/reshape | solution.py:95
  59.5 22.5 %all_to_all.29 = bf16[256,1,8,320]{3,2,1,0:T(8,128)(2,1)S(1)} all-to-all(bf16[256,1,8,320]{3,2,1,0:T(8,128)(2,1)S(1)} %copy.55), channel_id=1, replica_groups=mesh['mem'=4,'grid'=8] {'mem'}, dimensions={0} | all-to-all | bytes 2621440 | tf_op jit(solution)/shard_map/all_to_all | solution.py:96
  82.0 1.3 %copy.66 = bf16[64,4,1,8,320]{4,3,1,0,2:T(8,128)(2,1)} copy(bf16[64,4,1,8,320]{4,3,0,1,2:T(8,128)(2,1)S(1)} %bitcast.93) | data formatting | bytes 2621440 | tf_op jit(solution)/shard_map/all_to_all | solution.py:96
  (52 shorter events, 8.7 us)
Async XLA Ops:
  2.4 8.5 %collective-permute-start = (bf16[66,2,256]{2,0,1:T(8,128)(2,1)S(1)}, bf16[66,2,256]{2,0,1:T(8,128)(2,1)S(1)}, u32[]{:S(2)}, u32[]{:S(2)}) collective-permute-start(bf16[66,2,256]{2,0,1:T(8,128)(2,1)S(1)} %get-tuple-element.9), channel_id=1, source_target_pairs={{0,1},{1,2},{2,3},{3,4},{4,5},{5,6},{6,7},{7,0},{8,9},{9,10},{10,1... | collective-permute-start | bytes 202760 | tf_op jit(solution)/shard_map/ppermute | solution.py:20
  5.5 5.9 %collective-permute-start.1 = (bf16[66,2,256]{2,0,1:T(8,128)(2,1)S(1)}, bf16[66,2,256]{2,0,1:T(8,128)(2,1)S(1)}, u32[]{:S(2)}, u32[]{:S(2)}) collective-permute-start(bf16[66,2,256]{2,0,1:T(8,128)(2,1)S(1)} %get-tuple-element.10), channel_id=1, source_target_pairs={{1,0},{2,1},{3,2},{4,3},{5,4},{6,5},{7,6},{0,7},{9,8},{10,9},{11,1... | collective-permute-start | bytes 202760 | tf_op jit(solution)/shard_map/ppermute | solution.py:21
  13.6 4.4 %copy-start = (s32[4,4]{1,0:T(4,128)S(1)}, s32[4,4]{1,0:T(4,128)}, u32[]{:S(2)}) copy-start(s32[4,4]{1,0:T(4,128)} %param.10) | copy-start | bytes 196
  14.5 12.3 %all-to-all-start.1 = ((bf16[4,64,1,1,1024]{4,1,3,2,0:T(8,128)(2,1)}), bf16[4,64,1,1,1024]{4,1,3,2,0:T(8,128)(2,1)S(1)}, u32[]{:S(2)}, u32[]{:S(2)}) async-start(bf16[4,64,1,1,1024]{4,1,3,2,0:T(8,128)(2,1)} %pad_maximum_fusion), calls=%async_computation.1 | async-start | bytes 1048576 | tf_op jit(solution)/shard_map/all_to_all | solution.py:79
  26.8 23.6 %all-to-all-start = ((bf16[64,4,8,320]{3,2,0,1:T(8,128)(2,1)}), bf16[64,4,8,320]{3,2,0,1:T(8,128)(2,1)S(1)}, u32[]{:S(2)}, u32[]{:S(2)}) async-start(bf16[64,4,8,320]{3,2,0,1:T(8,128)(2,1)} %copy.49), calls=%async_computation | async-start | bytes 3145728 | tf_op jit(solution)/shard_map/all_to_all | solution.py:92
